TPU v7x, 32 devices: a whole 2x2x4 slice. The times are simulated.
32 devices in a mesh: dp: 8 (over z, x), tensor: 4 (over y, core).
Axes of the slice: x: 2, y: 2, z: 4, core: 2. Of those that a mesh axis runs over, the one named last changes fastest.
Arguments:
- tokens: bfloat16 [16, 512, 768], P('dp'), may hold values from -6 to 6
- lengths: int32 [16], P('dp'), may hold values from 1 to 512, 2048 in all
- groups: int32 [16, 512], P('dp'), may hold values from 0 to 3, never falling along the last dimension, each value on 1 to 256 neighbouring positions
- key_mask: int32 [16, 512], P('dp'), may hold values 0 or 1
- w_query: bfloat16 [768, 768], P(None, 'tensor'), may hold values from -0.21875 to 0.21875
- b_query: float32 [768], P('tensor'), may hold values from -3 to 3
- w_key: bfloat16 [768, 768], P(None, 'tensor'), may hold values from -0.21875 to 0.21875
- w_value: bfloat16 [768, 768], P(None, 'tensor'), may hold values from -0.21875 to 0.21875
- b_value: float32 [768], P('tensor'), may hold values from -3 to 3
- rel_bias: float32 [12, 256], P('tensor'), may hold values from -4 to 4
- w_out: bfloat16 [768, 768], P('tensor'), may hold values from -0.625 to 0.625
- b_out: float32 [768], replicated, may hold values from -3 to 3
- gain_one: float32 [768], replicated, may hold values from 0.25 to 1.75
- shift_one: float32 [768], replicated, may hold values from -3 to 3
- w_inner: bfloat16 [768, 3072], P(None, 'tensor'), may hold values from -0.21875 to 0.21875
- b_inner: float32 [3072], P('tensor'), may hold values from -3 to 3
- w_outer: bfloat16 [3072, 768], P('tensor'), may hold values from -0.109375 to 0.109375
- b_outer: float32 [768], replicated, may hold values from -3 to 3
- gain_two: float32 [768], replicated, may hold values from 0.25 to 1.75
- shift_two: float32 [768], replicated, may hold values from -3 to 3
- cotangent: bfloat16 [16, 256, 768], P('dp'), may hold values from -24 to 24
Outputs:
- output: bfloat16 [16, 256, 768], P('dp')
- grad_tokens: bfloat16 [16, 512, 768], P('dp')
- grad_w_query: float32 [768, 768], P(None, 'tensor')
- grad_b_query: float32 [768], P('tensor')
- grad_w_key: float32 [768, 768], P(None, 'tensor')
- grad_w_value: float32 [768, 768], P(None, 'tensor')
- grad_b_value: float32 [768], P('tensor')
- grad_rel_bias: float32 [12, 256], P('tensor')
- grad_w_out: float32 [768, 768], P('tensor')
- grad_b_out: float32 [768], replicated
- grad_gain_one: float32 [768], replicated
- grad_shift_one: float32 [768], replicated
- grad_w_inner: float32 [768, 3072], P(None, 'tensor')
- grad_b_inner: float32 [3072], P('tensor')
- grad_w_outer: float32 [3072, 768], P('tensor')
- grad_b_outer: float32 [768], replicated
- grad_gain_two: float32 [768], replicated
- grad_shift_two: float32 [768], replicated
Inputs may be any that keep to these rules, and one draw needn't show every extreme that they name: `lengths`: the longest row has exactly 512 used tokens. `groups`: document ids never fall along a row; a document has at most half of 512 positions.
All inputs are finite; a program needn't handle non-finite values. No bound on the sum of `lengths` or of `key_mask` on one device may be relied on, other than what follows from the above.
Results may differ from a plain program's by a relative error of at most 0.013.
Values sent between devices are 32-bit elements; how exact they have to be, the bound alone decides.
No kernel may reach another device: no remote copies, remote signals or barrier semaphores. Data moves between devices by JAX's collectives and lax.ppermute only.
A program may use at most 128 MiB of HBM per device.

v0:
```python
import jax
import jax.numpy as jnp
from jax import lax
from jax.sharding import PartitionSpec as P


def diagonal_table(seq, width):
    span = 2 * seq
    offset = jnp.arange(span, dtype=jnp.int32)
    distance = jnp.where(offset < seq, offset, offset - span)
    bucket = jnp.clip(distance, -(width // 2), width // 2 - 1) + width // 2
    return (bucket[:, None] == jnp.arange(width, dtype=jnp.int32)[None, :]).astype(jnp.float32)


def skewed_bias(rel_bias, onehot, half, seq):
    heads = rel_bias.shape[0]
    span = 2 * seq
    line = jnp.dot(rel_bias, onehot.T, precision=lax.Precision.HIGHEST)
    tiled = jnp.tile(line, (1, half))[:, : half * (span - 2)]
    return tiled.reshape(heads, half, span - 2)[:, :, :seq]


def skewed_bias_grad(score_sum, onehot, half, seq):
    heads = score_sum.shape[0]
    span = 2 * seq
    padded = jnp.pad(score_sum, ((0, 0), (0, 0), (0, span - 2 - seq))).reshape(
        heads, half * (span - 2)
    )
    padded = jnp.pad(padded, ((0, 0), (0, 2 * half))).reshape(heads, half, span)
    along = jnp.sum(padded, axis=1)
    return jnp.dot(along, onehot, precision=lax.Precision.HIGHEST)


def allowed_keys(lengths, groups, key_mask):
    seq = groups.shape[1]
    keyed = jnp.arange(seq, dtype=jnp.int32)
    own = groups[:, 0::2]
    same = own[:, :, None] == groups[:, None, :]
    live = (keyed[None, :] < lengths[:, None]) & (key_mask == 1)
    self_key = keyed[None, :] == 2 * jnp.arange(seq // 2, dtype=jnp.int32)[:, None]
    return same & live[:, None, :] | self_key[None]


def norm_forward(value, gain, shift):
    centre = value - jnp.mean(value, axis=-1, keepdims=True)
    spread = jnp.mean(centre * centre, axis=-1, keepdims=True)
    factor = lax.rsqrt(spread + 1e-05)
    normed = centre * factor
    return (normed * gain + shift, normed, factor)


def norm_backward(grad_out, normed, factor, gain):
    grad_norm = grad_out * gain
    first_mean = jnp.mean(grad_norm, axis=-1, keepdims=True)
    second_mean = jnp.mean(grad_norm * normed, axis=-1, keepdims=True)
    grad_in = factor * (grad_norm - first_mean - normed * second_mean)
    return (grad_in, jnp.sum(grad_out * normed, axis=(0, 1)), jnp.sum(grad_out, axis=(0, 1)))


def project(left, right):
    return jnp.einsum("rld,de->rle", left, right, preferred_element_type=jnp.float32)


def project_back(left, right):
    return jnp.einsum("rle,de->rld", left, right, preferred_element_type=jnp.float32)


def weight_grad(left, right):
    return jnp.einsum("rld,rle->de", left, right, preferred_element_type=jnp.float32)


def exact_gelu(value):
    return jax.nn.gelu(value, approximate=False)


def local(
    tokens,
    lengths,
    groups,
    key_mask,
    w_query,
    b_query,
    w_key,
    w_value,
    b_value,
    rel_bias,
    w_out,
    b_out,
    gain_one,
    shift_one,
    w_inner,
    b_inner,
    w_outer,
    b_outer,
    gain_two,
    shift_two,
    cotangent,
):
    rows, seq, width = tokens.shape
    half = seq // 2
    heads, table = rel_bias.shape
    head_dim = w_query.shape[1] // heads
    wide = tokens.astype(jnp.float32)
    pooled = jnp.sum(wide.reshape(rows, half, 2, width), axis=2) * 0.5
    pooled_low = pooled.astype(jnp.bfloat16)
    query = (project(pooled_low, w_query) + b_query).astype(jnp.bfloat16)
    keys = project(tokens, w_key).astype(jnp.bfloat16)
    values = (project(tokens, w_value) + b_value).astype(jnp.bfloat16)
    query_heads = query.reshape(rows, half, heads, head_dim)
    key_heads = keys.reshape(rows, seq, heads, head_dim)
    value_heads = values.reshape(rows, seq, heads, head_dim)
    onehot = diagonal_table(seq, table)
    bias = skewed_bias(rel_bias, onehot, half, seq)
    allowed = allowed_keys(lengths, groups, key_mask)[:, None]

    def masked_scores():
        raw = (
            jnp.einsum(
                "rqhe,rkhe->rhqk", query_heads, key_heads, preferred_element_type=jnp.float32
            )
            * 0.125
            + bias[None]
        )
        return jnp.where(allowed, raw, -1e30)

    scores = masked_scores()
    top = jnp.max(scores, axis=-1, keepdims=True)
    expo = jnp.exp(scores - top)
    total = jnp.sum(expo, axis=-1, keepdims=True)
    log_total = top + jnp.log(total)
    prob_low = (expo / total).astype(jnp.bfloat16)
    context = jnp.einsum(
        "rhqk,rkhe->rqhe", prob_low, value_heads, preferred_element_type=jnp.float32
    )
    context = context.astype(jnp.bfloat16).reshape(rows, half, heads * head_dim)
    attn = lax.psum(project(context, w_out), "tensor")
    first = pooled + (attn + b_out)
    y_one, normed_one, factor_one = norm_forward(first, gain_one, shift_one)
    y_low = y_one.astype(jnp.bfloat16)
    inner = project(y_low, w_inner) + b_inner
    act = exact_gelu(inner).astype(jnp.bfloat16)
    ffn = lax.psum(project(act, w_outer), "tensor")
    second = y_one + (ffn + b_outer)
    result, normed_two, factor_two = norm_forward(second, gain_two, shift_two)
    output = result.astype(jnp.bfloat16)
    grad_out = cotangent.astype(jnp.float32)
    grad_second, grad_gain_two, grad_shift_two = norm_backward(
        grad_out, normed_two, factor_two, gain_two
    )
    grad_b_outer = jnp.sum(grad_second, axis=(0, 1))
    grad_ffn = grad_second.astype(jnp.bfloat16)
    grad_w_outer = weight_grad(act, grad_ffn)
    grad_act = project_back(grad_ffn, w_outer)
    gelu_pull = jax.vjp(exact_gelu, inner)[1]
    grad_inner = gelu_pull(grad_act)[0].astype(jnp.bfloat16)
    grad_b_inner = jnp.sum(grad_inner.astype(jnp.float32), axis=(0, 1))
    grad_w_inner = weight_grad(y_low, grad_inner)
    grad_y = grad_second + lax.psum(project_back(grad_inner, w_inner), "tensor")
    grad_first, grad_gain_one, grad_shift_one = norm_backward(
        grad_y, normed_one, factor_one, gain_one
    )
    grad_b_out = jnp.sum(grad_first, axis=(0, 1))
    grad_attn = grad_first.astype(jnp.bfloat16)
    grad_w_out = weight_grad(context, grad_attn)
    grad_context = (
        project_back(grad_attn, w_out).astype(jnp.bfloat16).reshape(rows, half, heads, head_dim)
    )
    prob = jnp.exp(masked_scores() - log_total)
    grad_prob = jnp.einsum(
        "rqhe,rkhe->rhqk", grad_context, value_heads, preferred_element_type=jnp.float32
    )
    centre_term = jnp.sum(prob * grad_prob, axis=-1, keepdims=True)
    grad_scores = (prob * (grad_prob - centre_term)).astype(jnp.bfloat16)
    score_sum = jnp.sum(grad_scores.astype(jnp.float32), axis=0)
    grad_rel_bias = skewed_bias_grad(score_sum, onehot, half, seq)
    grad_query = (
        jnp.einsum("rhqk,rkhe->rqhe", grad_scores, key_heads, preferred_element_type=jnp.float32)
        * 0.125
    ).astype(jnp.bfloat16)
    grad_keys = (
        jnp.einsum("rhqk,rqhe->rkhe", grad_scores, query_heads, preferred_element_type=jnp.float32)
        * 0.125
    ).astype(jnp.bfloat16)
    grad_values = jnp.einsum(
        "rhqk,rqhe->rkhe", prob_low, grad_context, preferred_element_type=jnp.float32
    ).astype(jnp.bfloat16)
    grad_query = grad_query.reshape(rows, half, heads * head_dim)
    grad_keys = grad_keys.reshape(rows, seq, heads * head_dim)
    grad_values = grad_values.reshape(rows, seq, heads * head_dim)
    grad_b_query = jnp.sum(grad_query.astype(jnp.float32), axis=(0, 1))
    grad_b_value = jnp.sum(grad_values.astype(jnp.float32), axis=(0, 1))
    grad_w_query = weight_grad(pooled_low, grad_query)
    grad_w_key = weight_grad(tokens, grad_keys)
    grad_w_value = weight_grad(tokens, grad_values)
    pooled_part = project_back(grad_query, w_query)
    token_part = project_back(grad_keys, w_key) + project_back(grad_values, w_value)
    pooled_sum, token_sum = lax.psum((pooled_part, token_part), "tensor")
    grad_pooled = grad_first + pooled_sum
    grad_tokens = (token_sum + jnp.repeat(grad_pooled * 0.5, 2, axis=1)).astype(jnp.bfloat16)
    (
        grad_w_query,
        grad_b_query,
        grad_w_key,
        grad_w_value,
        grad_b_value,
        grad_rel_bias,
        grad_w_out,
        grad_b_out,
        grad_gain_one,
        grad_shift_one,
        grad_w_inner,
        grad_b_inner,
        grad_w_outer,
        grad_b_outer,
        grad_gain_two,
        grad_shift_two,
    ) = lax.psum(
        (
            grad_w_query,
            grad_b_query,
            grad_w_key,
            grad_w_value,
            grad_b_value,
            grad_rel_bias,
            grad_w_out,
            grad_b_out,
            grad_gain_one,
            grad_shift_one,
            grad_w_inner,
            grad_b_inner,
            grad_w_outer,
            grad_b_outer,
            grad_gain_two,
            grad_shift_two,
        ),
        "dp",
    )
    return (
        output,
        grad_tokens,
        grad_w_query,
        grad_b_query,
        grad_w_key,
        grad_w_value,
        grad_b_value,
        grad_rel_bias,
        grad_w_out,
        grad_b_out,
        grad_gain_one,
        grad_shift_one,
        grad_w_inner,
        grad_b_inner,
        grad_w_outer,
        grad_b_outer,
        grad_gain_two,
        grad_shift_two,
    )


def solution(mesh):
    placed = (
        P("dp", None, None),
        P("dp"),
        P("dp", None),
        P("dp", None),
        P(None, "tensor"),
        P("tensor"),
        P(None, "tensor"),
        P(None, "tensor"),
        P("tensor"),
        P("tensor", None),
        P("tensor", None),
        P(),
        P(),
        P(),
        P(None, "tensor"),
        P("tensor"),
        P("tensor", None),
        P(),
        P(),
        P(),
        P("dp", None, None),
    )
    return jax.shard_map(
        local,
        mesh=mesh,
        in_specs=placed,
        out_specs=(
            P("dp", None, None),
            P("dp", None, None),
            P(None, "tensor"),
            P("tensor"),
            P(None, "tensor"),
            P(None, "tensor"),
            P("tensor"),
            P("tensor", None),
            P("tensor", None),
            P(),
            P(),
            P(),
            P(None, "tensor"),
            P("tensor"),
            P("tensor", None),
            P(),
            P(),
            P(),
        ),
        check_vma=False,
    )
```

profile of v0, /device:TPU:0, one launch (start us, length us, event | category | flops | bytes accessed | tf_op | source)
XLA Modules:
  0.0 569.8 jit_solution(7469340155090265146)
XLA Ops:
  9.1 5.0 reshape.201
  18.0 2.8 slice.12
  20.8 7.5 %reshape.191 = f32[3,256,1022]{2,1,0:T(8,128)} reshape(f32[3,261632]{1,0:T(4,128)} %slice.12) | data formatting | bytes 6279168 | tf_op jit(solution)/shard_map/reshape | solution.py:20
  29.1 5.6 reduce_sum.202
  44.7 45.5 %all-reduce.11.cloned.1.call-done = f32[2,256,768]{2,1,0:T(8,128)} async-done(((f32[2,256,768]{2,1,0:T(8,128)}), f32[2,256,768]{2,1,0:T(8,128)}) %all-reduce.11.cloned.1.call-update) | async-done | bytes 1572880 | tf_op jit(solution)/shard_map/psum | solution.py:136
  90.2 2.2 fusion.59
  94.3 4.5 multiply_convert_fusion.1
  101.6 43.0 %all-reduce.13.cloned.1.call-done = f32[2,256,768]{2,1,0:T(8,128)} async-done(((f32[2,256,768]{2,1,0:T(8,128)}), f32[2,256,768]{2,1,0:T(8,128)}) %all-reduce.13.cloned.1.call-update) | async-done | bytes 1572880 | tf_op jit(solution)/shard_map/psum | solution.py:142
  149.4 2.2 convert_reduce_fusion.2
  155.3 42.4 %all-reduce.15.cloned.1.call-done = f32[2,256,768]{2,1,0:T(8,128)} async-done(((f32[2,256,768]{2,1,0:T(8,128)}), f32[2,256,768]{2,1,0:T(8,128)}) %all-reduce.15.cloned.1.call-update) | async-done | bytes 1572880 | tf_op jit(solution)/shard_map/psum | solution.py:158
  197.7 4.6 fusion.8
  207.1 2.2 convert_reduce_fusion
  214.0 2.4 convolution_add_fusion
  217.2 3.7 convolution_bitcast_fusion.1
  220.9 2.5 convolution_bitcast_fusion
  230.1 3.6 pad.8
  233.7 7.6 %reshape.198 = f32[3,261632]{1,0:T(4,128)} reshape(f32[3,256,1022]{2,1,0:T(8,128)} %pad.8) | data formatting | bytes 6279168 | tf_op jit(solution)/shard_map/reshape | solution.py:26
  241.3 2.7 pad.9
  246.3 38.5 %all-reduce.2 = (f32[192]{0:T(256)}, f32[192]{0:T(256)}, f32[3,256]{1,0:T(4,128)}, f32[768]{0:T(1024)}, f32[768]{0:T(1024)}, /*index=5*/f32[768]{0:T(1024)}, f32...) all-reduce(f32[192]{0:T(256)S(1)} %reduce_sum.214, ...), channel_id=1, replica_groups=mesh['dp'=8,'tensor'=4] {'dp'}, use_global_device_ids=true, to_apply=%region_19.20 | all-reduce | flops 6528 | bytes 52224 | tf_op jit(solution)/shard_map/psum | solution.py:217
  284.8 26.1 %all-reduce.19.cloned.1.call-done = (f32[2,512,768]{2,1,0:T(8,128)}, f32[2,256,768]{2,1,0:T(8,128)}) async-done(((f32[2,512,768]{2,1,0:T(8,128)}, f32[2,256,768]{2,1,0:T(8,128)}), (f32[2,512,768]{2,1,0:T(8,128)}, f32[2,256,768]{2,1,0:T(8,128)})) %all-reduce.19.cloned.1.call-update) | async-done | bytes 4718608 | tf_op jit(solution)/shard_map/psum | solution.py:197
  312.5 2.8 broadcast_in_dim.16
  315.3 5.3 reshape.197
  320.6 5.1 add_convert_fusion
  325.6 228.9 %all-reduce.17.cloned.1.call-done = (f32[768,192]{0,1:T(8,128)}, f32[768,192]{0,1:T(8,128)}, f32[768,192]{0,1:T(8,128)}, f32[192,768]{1,0:T(8,128)}, f32[768,768]{1,0:T(8,128)}, /*index=5*/f32[768,768]{1,0:T(8,128)}) async-done(((f32[768,192]{0,1:T(8,128)}, f32[768,192]{0,1:T(8,128)}, f32[768,192]{0,1:T(8,128)}, f32[192,768]{1,0:T(8,128)}, f32[768,768]{1,0:T(8,128)}, /*index=5*/f32[768,768]{1,0:T(8,128)}), ...) | async-done | bytes 7077904 | tf_op jit(solution)/shard_map/psum | solution.py:217
  (251 shorter events, 58.3 us)
Async XLA Ops:
  7.2 85.5 %copy-start = (bf16[768,768]{1,0:T(8,128)(2,1)S(1)}, bf16[768,768]{1,0:T(8,128)(2,1)}, u32[]{:S(2)}) copy-start(bf16[768,768]{1,0:T(8,128)(2,1)} %param.35) | copy-start | bytes 3538948
  7.2 83.0 %all-reduce.11.cloned.1.call-start = ((), (), s32[]{:S(2)}) async-start(), calls=%async_computation | async-start | bytes 3145728 | tf_op jit(solution)/shard_map/psum | solution.py:136
  7.3 7.5 %copy-start.78 = (s32[1024]{0:T(1024)}, s32[1024]{0:T(1024)S(1)}, u32[]{:S(2)}) copy-start(s32[1024]{0:T(1024)S(1)} %fusion.48) | copy-start | bytes 12292
  14.8 21.9 %copy-start.25 = (bf16[2,512,192]{1,2,0:T(8,128)(2,1)}, bf16[2,512,192]{1,2,0:T(8,128)(2,1)S(1)}, u32[]{:S(2)}) copy-start(bf16[2,512,192]{1,2,0:T(8,128)(2,1)S(1)} %convolution_convert_fusion.1) | copy-start | bytes 1179652
  29.1 5.7 copy-start.66
  29.1 7.1 %copy-start.29 = (bf16[768,192]{0,1:T(8,128)(2,1)S(1)}, bf16[768,192]{0,1:T(8,128)(2,1)}, u32[]{:S(2)}) copy-start(bf16[768,192]{0,1:T(8,128)(2,1)} %param.25) | copy-start | bytes 884740
  29.1 7.2 %copy-start.84 = (f32[192]{0:T(256)S(1)}, f32[192]{0:T(256)}, u32[]{:S(2)}) copy-start(f32[192]{0:T(256)} %param.26) | copy-start | bytes 2308
  42.9 47.3 %copy-start.75 = (f32[768]{0:T(1024)S(1)}, f32[768]{0:T(1024)}, u32[]{:S(2)}) copy-start(f32[768]{0:T(1024)} %param.32) | copy-start | bytes 9220
  44.5 100.2 %all-reduce.13.cloned.1.call-start = ((), (), s32[]{:S(2)}) async-start(), calls=%async_computation.1 | async-start | bytes 3145728 | tf_op jit(solution)/shard_map/psum | solution.py:142
  92.4 52.3 %copy-start.43 = (f32[2,256]{1,0:T(2,128)}, f32[2,256]{1,0:T(2,128)S(1)}, u32[]{:S(2)}) copy-start(f32[2,256]{1,0:T(2,128)S(1)} %broadcast_multiply_fusion.5) | copy-start | bytes 6148
  93.1 51.6 %copy-start.49 = (f32[2,256]{1,0:T(2,128)}, f32[2,256]{1,0:T(2,128)S(1)}, u32[]{:S(2)}) copy-start(f32[2,256]{1,0:T(2,128)S(1)} %add_rsqrt_fusion.1) | copy-start | bytes 6148
  101.6 43.1 %copy-start.81 = (f32[768]{0:T(1024)S(1)}, f32[768]{0:T(1024)}, u32[]{:S(2)}) copy-start(f32[768]{0:T(1024)} %param.38) | copy-start | bytes 9220
  101.6 96.1 %all-reduce.15.cloned.1.call-start = ((), (), s32[]{:S(2)}) async-start(), calls=%async_computation.2 | async-start | bytes 3145728 | tf_op jit(solution)/shard_map/psum | solution.py:158
  154.5 43.2 %copy-start.44 = (f32[2,256]{1,0:T(2,128)S(1)}, f32[2,256]{1,0:T(2,128)}, u32[]{:S(2)}) copy-start(f32[2,256]{1,0:T(2,128)} %copy-done.43) | copy-start | bytes 6148
  154.5 43.2 %copy-start.47 = (f32[768]{0:T(1024)S(1)}, f32[768]{0:T(1024)}, u32[]{:S(2)}) copy-start(f32[768]{0:T(1024)} %param.33) | copy-start | bytes 9220
  154.5 43.2 %copy-start.50 = (f32[2,256]{1,0:T(2,128)S(1)}, f32[2,256]{1,0:T(2,128)}, u32[]{:S(2)}) copy-start(f32[2,256]{1,0:T(2,128)} %copy-done.49) | copy-start | bytes 6148
  154.5 43.2 %copy-start.53 = (f32[2,256]{1,0:T(2,128)S(1)}, f32[2,256]{1,0:T(2,128)}, u32[]{:S(2)}) copy-start(f32[2,256]{1,0:T(2,128)} %copy-done.52) | copy-start | bytes 6148
  154.5 43.2 %copy-start.56 = (f32[2,256]{1,0:T(2,128)S(1)}, f32[2,256]{1,0:T(2,128)}, u32[]{:S(2)}) copy-start(f32[2,256]{1,0:T(2,128)} %copy-done.55) | copy-start | bytes 6148
  154.5 43.2 %copy-start.59 = (f32[768]{0:T(1024)S(1)}, f32[768]{0:T(1024)}, u32[]{:S(2)}) copy-start(f32[768]{0:T(1024)} %param.39) | copy-start | bytes 9220
  154.5 43.2 %copy-start.70 = (f32[2,256]{1,0:T(2,128)S(1)}, f32[2,256]{1,0:T(2,128)}, u32[]{:S(2)}) copy-start(f32[2,256]{1,0:T(2,128)} %copy-done.69) | copy-start | bytes 6148
  154.6 43.2 %copy-start.73 = (f32[2,256]{1,0:T(2,128)S(1)}, f32[2,256]{1,0:T(2,128)}, u32[]{:S(2)}) copy-start(f32[2,256]{1,0:T(2,128)} %copy-done.72) | copy-start | bytes 6148
  154.6 43.2 %copy-start.76 = (f32[768]{0:T(1024)S(1)}, f32[768]{0:T(1024)}, u32[]{:S(2)}) copy-start(f32[768]{0:T(1024)} %param.40) | copy-start | bytes 9220
  154.6 156.2 %all-reduce.19.cloned.1.call-start = ((), (), s32[]{:S(2)}) async-start(), calls=%async_computation.4 | async-start | bytes 9437184 | tf_op jit(solution)/shard_map/psum | solution.py:197
  216.5 338.0 %all-reduce.17.cloned.1.call-start = ((), (), s32[]{:S(2)}) async-start(), calls=%async_computation.3 | async-start | bytes 14155776 | tf_op jit(solution)/shard_map/psum | solution.py:217
  (74 other events, 159.4 us)
Sparse Core Ops, SparseCore 0:
  44.6 45.5 all-reduce.10
  101.7 42.8 all-reduce.12
  154.7 42.8 all-reduce.14
  216.6 94.2 all-reduce.18
  316.9 237.5 all-reduce.16
where the time goes:
time: 575 us; the launch traced here: 570 us
  waiting for transfers between devices  386 us (67%)
  local copies, waits for them, and re-layouts  60.4 us (11%)
  blocking collectives  38.5 us (7%)
  other arithmetic  36.3 us (6%)
  matrix products  33.2 us (6%)
  between operations  14.9 us (3%)
    psum x1, waiting for transfers between devices, local(): lax.psum((grad_w_query, grad_b_query, grad_w_key, grad_w_value, grad_b_va...  229 us
    psum x1, waiting for transfers between devices, local(): attn = lax.psum(project(context, w_out), 'tensor')  45.5 us
    psum x1, waiting for transfers between devices, local(): ffn = lax.psum(project(act, w_outer), 'tensor')  43 us
    psum x1, waiting for transfers between devices, local(): grad_y = grad_second + lax.psum(project_back(grad_inner, w_inner), 'tensor')  42.4 us
    psum x1, blocking collectives, local(): lax.psum((grad_w_query, grad_b_query, grad_w_key, grad_w_value, grad_b_va...  38.5 us
    psum x1, waiting for transfers between devices, local(): pooled_sum, token_sum = lax.psum((pooled_part, token_part), 'tensor')  26.1 us
    unnamed x192, local copies, waits for them, and re-layouts  21.8 us
  transfers between devices with their start and end apart: 5, of which 5 were waited for; matrix products, arithmetic and copies ran while one was open for 7% of the time, Pallas kernels for 0%

commit v1 on v0

--- a/solution.py
+++ b/solution.py
@@ -133,7 +133,7 @@
         "rhqk,rkhe->rqhe", prob_low, value_heads, preferred_element_type=jnp.float32
     )
     context = context.astype(jnp.bfloat16).reshape(rows, half, heads * head_dim)
-    attn = lax.psum(project(context, w_out), "tensor")
+    attn = jnp.sum(lax.all_gather(project(context, w_out), "tensor"), axis=0)
     first = pooled + (attn + b_out)
     y_one, normed_one, factor_one = norm_forward(first, gain_one, shift_one)
     y_low = y_one.astype(jnp.bfloat16)

time: 575 us -> 583 us (1.014)
    all_gather x0 -> x1, waiting for transfers between devices: none -> 49 us  [local(): attn = jnp.sum(lax.all_gather(project(context, w_out), 'tensor'), axis=0)]
    psum x1 -> x0, waiting for transfers between devices: 45.5 us -> none  [local(): attn = lax.psum(project(context, w_out), 'tensor')]
where the time goes in v1:
time: 583 us; the launch traced here: 578 us
  waiting for transfers between devices  389 us (67%)
  local copies, waits for them, and re-layouts  60.4 us (10%)
  other arithmetic  40.8 us (7%)
  blocking collectives  38.5 us (7%)
  matrix products  33.2 us (6%)
  between operations  14.9 us (3%)
    psum x1, waiting for transfers between devices, local(): lax.psum((grad_w_query, grad_b_query, grad_w_key, grad_w_value, grad_b_va...  229 us
    all_gather x1, waiting for transfers between devices, local(): attn = jnp.sum(lax.all_gather(project(context, w_out), 'tensor'), axis=0)  49 us
    psum x1, waiting for transfers between devices, local(): ffn = lax.psum(project(act, w_outer), 'tensor')  43 us
    psum x1, waiting for transfers between devices, local(): grad_y = grad_second + lax.psum(project_back(grad_inner, w_inner), 'tensor')  42.4 us
    psum x1, blocking collectives, local(): lax.psum((grad_w_query, grad_b_query, grad_w_key, grad_w_value, grad_b_va...  38.5 us
    psum x1, waiting for transfers between devices, local(): pooled_sum, token_sum = lax.psum((pooled_part, token_part), 'tensor')  26.1 us
    unnamed x192, local copies, waits for them, and re-layouts  21.9 us
  transfers between devices with their start and end apart: 5, of which 5 were waited for; matrix products, arithmetic and copies ran while one was open for 7% of the time, Pallas kernels for 0%

profile of v1, /device:TPU:0, one launch (start us, length us, event | category | flops | bytes accessed | tf_op | source)
XLA Modules:
  0.0 577.8 jit_solution(13805171496610927688)
XLA Ops:
  9.1 5.0 reshape.201
  18.0 2.8 slice.12
  20.8 7.5 %reshape.191 = f32[3,256,1022]{2,1,0:T(8,128)} reshape(f32[3,261632]{1,0:T(4,128)} %slice.12) | data formatting | bytes 6279168 | tf_op jit(solution)/shard_map/reshape | solution.py:20
  29.1 5.6 reduce_sum.211
  44.8 49.0 %all-gather.3.cloned.1.call-done = f32[8,256,768]{2,1,0:T(8,128)} async-done(((f32[2,256,768]{2,1,0:T(8,128)}), f32[8,256,768]{2,1,0:T(8,128)}) %all-gather.3.cloned.1.call-update) | async-done | bytes 6291472 | tf_op jit(solution)/shard_map/all_gather | solution.py:136
  93.8 4.5 reduce_sum.213
  102.4 4.5 multiply_convert_fusion.1
  109.8 43.0 %all-reduce.10.cloned.1.call-done = f32[2,256,768]{2,1,0:T(8,128)} async-done(((f32[2,256,768]{2,1,0:T(8,128)}), f32[2,256,768]{2,1,0:T(8,128)}) %all-reduce.10.cloned.1.call-update) | async-done | bytes 1572880 | tf_op jit(solution)/shard_map/psum | solution.py:142
  157.5 2.2 convert_reduce_fusion.2
  163.3 42.4 %all-reduce.12.cloned.1.call-done = f32[2,256,768]{2,1,0:T(8,128)} async-done(((f32[2,256,768]{2,1,0:T(8,128)}), f32[2,256,768]{2,1,0:T(8,128)}) %all-reduce.12.cloned.1.call-update) | async-done | bytes 1572880 | tf_op jit(solution)/shard_map/psum | solution.py:158
  205.8 4.6 fusion.8
  215.2 2.2 convert_reduce_fusion
  222.1 2.4 convolution_add_fusion
  225.2 3.7 convolution_bitcast_fusion.1
  229.0 2.5 convolution_bitcast_fusion
  238.2 3.6 pad.8
  241.8 7.6 %reshape.198 = f32[3,261632]{1,0:T(4,128)} reshape(f32[3,256,1022]{2,1,0:T(8,128)} %pad.8) | data formatting | bytes 6279168 | tf_op jit(solution)/shard_map/reshape | solution.py:26
  249.4 2.7 pad.9
  254.3 38.5 %all-reduce.2 = (f32[192]{0:T(256)}, f32[192]{0:T(256)}, f32[3,256]{1,0:T(4,128)}, f32[768]{0:T(1024)}, f32[768]{0:T(1024)}, /*index=5*/f32[768]{0:T(1024)}, f32...) all-reduce(f32[192]{0:T(256)S(1)} %reduce_sum.224, ...), channel_id=1, replica_groups=mesh['dp'=8,'tensor'=4] {'dp'}, use_global_device_ids=true, to_apply=%region_19.20 | all-reduce | flops 6528 | bytes 52224 | tf_op jit(solution)/shard_map/psum | solution.py:217
  292.8 26.1 %all-reduce.16.cloned.1.call-done = (f32[2,512,768]{2,1,0:T(8,128)}, f32[2,256,768]{2,1,0:T(8,128)}) async-done(((f32[2,512,768]{2,1,0:T(8,128)}, f32[2,256,768]{2,1,0:T(8,128)}), (f32[2,512,768]{2,1,0:T(8,128)}, f32[2,256,768]{2,1,0:T(8,128)})) %all-reduce.16.cloned.1.call-update) | async-done | bytes 4718608 | tf_op jit(solution)/shard_map/psum | solution.py:197
  320.5 2.8 broadcast_in_dim.16
  323.4 5.3 reshape.197
  328.6 5.1 add_convert_fusion
  333.7 228.9 %all-reduce.14.cloned.1.call-done = (f32[768,192]{0,1:T(8,128)}, f32[768,192]{0,1:T(8,128)}, f32[768,192]{0,1:T(8,128)}, f32[192,768]{1,0:T(8,128)}, f32[768,768]{1,0:T(8,128)}, /*index=5*/f32[768,768]{1,0:T(8,128)}) async-done(((f32[768,192]{0,1:T(8,128)}, f32[768,192]{0,1:T(8,128)}, f32[768,192]{0,1:T(8,128)}, f32[192,768]{1,0:T(8,128)}, f32[768,768]{1,0:T(8,128)}, /*index=5*/f32[768,768]{1,0:T(8,128)}), ...) | async-done | bytes 7077904 | tf_op jit(solution)/shard_map/psum | solution.py:217
  (252 shorter events, 60.5 us)
Async XLA Ops:
  7.2 93.7 %copy-start = (bf16[768,768]{1,0:T(8,128)(2,1)S(1)}, bf16[768,768]{1,0:T(8,128)(2,1)}, u32[]{:S(2)}) copy-start(bf16[768,768]{1,0:T(8,128)(2,1)} %param.35) | copy-start | bytes 3538948
  7.2 86.6 %all-gather.3.cloned.1.call-start = ((), (), s32[]{:S(2)}) async-start(), calls=%async_computation.2 | async-start | bytes 7864320 | tf_op jit(solution)/shard_map/all_gather | solution.py:136
  7.3 7.5 %copy-start.78 = (s32[1024]{0:T(1024)}, s32[1024]{0:T(1024)S(1)}, u32[]{:S(2)}) copy-start(s32[1024]{0:T(1024)S(1)} %fusion.48) | copy-start | bytes 12292
  14.8 21.9 %copy-start.25 = (bf16[2,512,192]{1,2,0:T(8,128)(2,1)}, bf16[2,512,192]{1,2,0:T(8,128)(2,1)S(1)}, u32[]{:S(2)}) copy-start(bf16[2,512,192]{1,2,0:T(8,128)(2,1)S(1)} %convolution_convert_fusion.1) | copy-start | bytes 1179652
  29.1 5.7 copy-start.66
  29.1 7.1 %copy-start.29 = (bf16[768,192]{0,1:T(8,128)(2,1)S(1)}, bf16[768,192]{0,1:T(8,128)(2,1)}, u32[]{:S(2)}) copy-start(bf16[768,192]{0,1:T(8,128)(2,1)} %param.25) | copy-start | bytes 884740
  29.1 7.2 %copy-start.84 = (f32[192]{0:T(256)S(1)}, f32[192]{0:T(256)}, u32[]{:S(2)}) copy-start(f32[192]{0:T(256)} %param.26) | copy-start | bytes 2308
  44.6 108.2 %all-reduce.10.cloned.1.call-start = ((), (), s32[]{:S(2)}) async-start(), calls=%async_computation | async-start | bytes 3145728 | tf_op jit(solution)/shard_map/psum | solution.py:142
  100.5 52.2 %copy-start.43 = (f32[2,256]{1,0:T(2,128)}, f32[2,256]{1,0:T(2,128)S(1)}, u32[]{:S(2)}) copy-start(f32[2,256]{1,0:T(2,128)S(1)} %broadcast_multiply_fusion.5) | copy-start | bytes 6148
  101.2 51.5 %copy-start.49 = (f32[2,256]{1,0:T(2,128)}, f32[2,256]{1,0:T(2,128)S(1)}, u32[]{:S(2)}) copy-start(f32[2,256]{1,0:T(2,128)S(1)} %add_rsqrt_fusion.1) | copy-start | bytes 6148
  102.4 5.3 copy-start.86
  109.7 43.0 %copy-start.81 = (f32[768]{0:T(1024)S(1)}, f32[768]{0:T(1024)}, u32[]{:S(2)}) copy-start(f32[768]{0:T(1024)} %param.38) | copy-start | bytes 9220
  109.7 96.0 %all-reduce.12.cloned.1.call-start = ((), (), s32[]{:S(2)}) async-start(), calls=%async_computation.1 | async-start | bytes 3145728 | tf_op jit(solution)/shard_map/psum | solution.py:158
  162.6 43.2 %copy-start.44 = (f32[2,256]{1,0:T(2,128)S(1)}, f32[2,256]{1,0:T(2,128)}, u32[]{:S(2)}) copy-start(f32[2,256]{1,0:T(2,128)} %copy-done.43) | copy-start | bytes 6148
  162.6 43.2 %copy-start.47 = (f32[768]{0:T(1024)S(1)}, f32[768]{0:T(1024)}, u32[]{:S(2)}) copy-start(f32[768]{0:T(1024)} %param.33) | copy-start | bytes 9220
  162.6 43.2 %copy-start.50 = (f32[2,256]{1,0:T(2,128)S(1)}, f32[2,256]{1,0:T(2,128)}, u32[]{:S(2)}) copy-start(f32[2,256]{1,0:T(2,128)} %copy-done.49) | copy-start | bytes 6148
  162.6 43.2 %copy-start.53 = (f32[2,256]{1,0:T(2,128)S(1)}, f32[2,256]{1,0:T(2,128)}, u32[]{:S(2)}) copy-start(f32[2,256]{1,0:T(2,128)} %copy-done.52) | copy-start | bytes 6148
  162.6 43.2 %copy-start.56 = (f32[2,256]{1,0:T(2,128)S(1)}, f32[2,256]{1,0:T(2,128)}, u32[]{:S(2)}) copy-start(f32[2,256]{1,0:T(2,128)} %copy-done.55) | copy-start | bytes 6148
  162.6 43.2 %copy-start.59 = (f32[768]{0:T(1024)S(1)}, f32[768]{0:T(1024)}, u32[]{:S(2)}) copy-start(f32[768]{0:T(1024)} %param.39) | copy-start | bytes 9220
  162.6 43.2 %copy-start.70 = (f32[2,256]{1,0:T(2,128)S(1)}, f32[2,256]{1,0:T(2,128)}, u32[]{:S(2)}) copy-start(f32[2,256]{1,0:T(2,128)} %copy-done.69) | copy-start | bytes 6148
  162.6 43.2 %copy-start.73 = (f32[2,256]{1,0:T(2,128)S(1)}, f32[2,256]{1,0:T(2,128)}, u32[]{:S(2)}) copy-start(f32[2,256]{1,0:T(2,128)} %copy-done.72) | copy-start | bytes 6148
  162.6 43.2 %copy-start.76 = (f32[768]{0:T(1024)S(1)}, f32[768]{0:T(1024)}, u32[]{:S(2)}) copy-start(f32[768]{0:T(1024)} %param.40) | copy-start | bytes 9220
  162.7 156.3 %all-reduce.16.cloned.1.call-start = ((), (), s32[]{:S(2)}) async-start(), calls=%async_computation.4 | async-start | bytes 9437184 | tf_op jit(solution)/shard_map/psum | solution.py:197
  224.5 338.1 %all-reduce.14.cloned.1.call-start = ((), (), s32[]{:S(2)}) async-start(), calls=%async_computation.3 | async-start | bytes 14155776 | tf_op jit(solution)/shard_map/psum | solution.py:217
  (74 other events, 158.5 us)
Sparse Core Ops, SparseCore 0:
  44.7 49.0 all-gather.2
  109.8 42.8 all-reduce.9
  162.8 42.8 all-reduce.11
  224.6 94.2 all-reduce.15
  325.0 237.5 all-reduce.13
